TPU v7x, 32 devices: a whole 2x2x4 slice. The times are simulated.
32 devices in a mesh: span: 16 (over z, x, core), qry: 2 (over y).
Axes of the slice: x: 2, y: 2, z: 4, core: 2. Of those that a mesh axis runs over, the one named last changes fastest.
Arguments:
- features: bfloat16 [16, 4, 128, 256], P('span', 'qry'), may hold values from -6 to 6
- conv_weight: bfloat16 [27, 256, 256], replicated, may hold values from -0.078125 to 0.078125
- queries: float32 [16, 256], P('qry'), may hold values from -600 to 600
- w_query: bfloat16 [2, 256, 256], replicated, may hold values from -0.26171875 to 0.26171875
- w_key: bfloat16 [2, 256, 256], replicated, may hold values from -0.26171875 to 0.26171875
- w_value: bfloat16 [2, 256, 256], replicated, may hold values from -0.26171875 to 0.26171875
- w_out: bfloat16 [2, 256, 256], replicated, may hold values from -0.26171875 to 0.26171875
- norm_gain: float32 [256], replicated, may hold values from 0.5 to 1.5
- mask_weight: bfloat16 [256, 256], replicated, may hold values from -0.375 to 0.375
- mask_blocks: int32 [16, 4], replicated, may hold values from 0 to 63, as said below
Outputs:
- query_embed: float32 [16, 256], P('qry')
- mask_logits: bfloat16 [16, 16, 4, 128], P(None, 'span', 'qry')
Inputs may be any that keep to these rules, and one draw needn't show every extreme that they name: `mask_blocks`: each row lists 4 distinct mask blocks, block z * 4 + y being the voxels pixel[z, y, :]; no block appears twice in the whole array.
All inputs are finite; a program needn't handle non-finite values.
Results may differ from a plain program's by a relative error of at most 0.04.
The roundings to bfloat16 on the way count: a program that leaves them out, or rounds other values in their place, can miss the bound.
Values may be sent and summed in bfloat16 or wider, within the bound.
No kernel may reach another device: no remote copies, remote signals or barrier semaphores. Data moves between devices by JAX's collectives and lax.ppermute only.
A program may use at most 64 MiB of HBM per device.

v0:
```python
import jax
import jax.numpy as jnp
from jax import lax
from jax.sharding import PartitionSpec as P

HEADS = 8
LAYERS = 2


def with_halo(cells, sides, width):
    for axis, dim in sides:
        count = lax.axis_size(axis)
        ends = count - 1
        head = lax.slice_in_dim(cells, 0, width, axis=dim)
        tail = lax.slice_in_dim(cells, cells.shape[dim] - width, cells.shape[dim], axis=dim)
        cells = jnp.concatenate(
            [
                lax.ppermute(tail, axis, [(i, (i + 1) % count) for i in range(ends)]),
                cells,
                lax.ppermute(head, axis, [((i + 1) % count, i) for i in range(ends)]),
            ],
            axis=dim,
        )
    return cells


def merged(value, axis, join):
    pieces = jax.tree.map(lambda part: lax.all_gather(part, axis), value)
    head = jax.tree.map(lambda part: part[0], pieces)
    tail = jax.tree.map(lambda part: part[1:], pieces)
    so_far, _ = lax.scan(lambda so_far, piece: (join(so_far, piece), None), head, tail)
    return so_far


def combine_parts(first_part, second_part):
    first_top, first_total, first_sum = first_part
    second_top, second_total, second_sum = second_part
    merged_top = jnp.maximum(first_top, second_top)
    first_factor = jnp.exp(first_top - merged_top)
    second_factor = jnp.exp(second_top - merged_top)
    merged_total = first_total * first_factor + second_total * second_factor
    merged_sum = first_sum * first_factor[..., None] + second_sum * second_factor[..., None]
    return (merged_top, merged_total, merged_sum)


def normalize(state, norm_gain):
    mean = jnp.mean(state, axis=-1, keepdims=True)
    centered = state - mean
    var = jnp.mean(centered * centered, axis=-1, keepdims=True)
    return centered * lax.rsqrt(var + 1e-05) * norm_gain


def local(
    features,
    conv_weight,
    queries,
    w_query,
    w_key,
    w_value,
    w_out,
    norm_gain,
    mask_weight,
    mask_blocks,
):
    depth_cells, row_cells, x_cells, channels = features.shape
    extended = with_halo(features, (("span", 0), ("qry", 1)), 1)
    padded = jnp.pad(extended, ((0, 0), (0, 0), (1, 1), (0, 0)))
    taps = conv_weight.reshape(3, 3, 3, channels, channels)
    conv = jnp.zeros((depth_cells, row_cells, x_cells, channels), jnp.float32)
    for depth_off in range(3):
        for row_off in range(3):
            slab = padded[
                depth_off : depth_off + depth_cells, row_off : row_off + row_cells
            ].reshape(-1, channels)
            wide_taps = jnp.concatenate(
                [
                    taps[depth_off, row_off, 0],
                    taps[depth_off, row_off, 1],
                    taps[depth_off, row_off, 2],
                ],
                axis=1,
            )
            product = jnp.dot(slab, wide_taps, preferred_element_type=jnp.float32)
            product = product.reshape(depth_cells, row_cells, x_cells + 2, 3, channels)
            conv = (
                conv
                + product[:, :, 0:x_cells, 0]
                + product[:, :, 1 : x_cells + 1, 1]
                + product[:, :, 2 : x_cells + 2, 2]
            )
    pixel = jnp.maximum(conv, 0.0).astype(jnp.bfloat16)
    voxels = depth_cells * row_cells * x_cells
    local_blocks = depth_cells * row_cells
    flat = pixel.reshape(voxels, channels)
    grid_rows = row_cells * lax.axis_size("qry")
    depth_ids = lax.axis_index("span") * depth_cells + jnp.arange(depth_cells, dtype=jnp.int32)
    row_ids = lax.axis_index("qry") * row_cells + jnp.arange(row_cells, dtype=jnp.int32)
    block_ids = (depth_ids[:, None] * grid_rows + row_ids[None, :]).reshape(-1)
    matches = mask_blocks[:, :, None] == block_ids[None, None, :]
    present = jnp.any(matches, axis=1)
    query_count = mask_blocks.shape[0]
    head_dim = channels // HEADS
    scale = head_dim ** (-0.5)
    query_group = 64 if query_count % 64 == 0 else query_count
    state = queries
    for layer_index in range(LAYERS):
        state_all = lax.all_gather(state, "qry", axis=0, tiled=True)
        qproj = (
            (
                jnp.dot(
                    state_all.astype(jnp.bfloat16),
                    w_query[layer_index],
                    preferred_element_type=jnp.float32,
                )
                * scale
            )
            .astype(jnp.bfloat16)
            .reshape(query_count // query_group, query_group, HEADS, head_dim)
        )
        keys = jnp.dot(flat, w_key[layer_index], preferred_element_type=jnp.float32).astype(
            jnp.bfloat16
        )
        values = jnp.dot(flat, w_value[layer_index], preferred_element_type=jnp.float32).astype(
            jnp.bfloat16
        )
        partial_keys = keys
        partial_values = values
        partial_keys = partial_keys.reshape(voxels, HEADS, head_dim)
        partial_values = partial_values.reshape(voxels, HEADS, head_dim)
        present_groups = present.reshape(query_count // query_group, query_group, local_blocks)

        def one_group(operands):
            group_q, group_present = operands
            allowed = jnp.broadcast_to(
                group_present[:, None, :, None], (query_group, 1, local_blocks, x_cells)
            ).reshape(query_group, 1, voxels)
            scores = jnp.einsum(
                "nhe,vhe->nhv", group_q, partial_keys, preferred_element_type=jnp.float32
            )
            local_top = jnp.max(jnp.where(allowed, scores, -1e30), axis=-1)
            prob = jnp.where(allowed, jnp.exp(scores - local_top[..., None]), 0.0)
            local_total = jnp.sum(prob, axis=-1)
            local_sum = jnp.einsum(
                "nhv,vhe->nhe",
                prob.astype(jnp.bfloat16),
                partial_values,
                preferred_element_type=jnp.float32,
            )
            return (local_top, local_total, local_sum)

        group_top, group_total, group_sum = lax.map(one_group, (qproj, present_groups))
        local_top = group_top.reshape(query_count, HEADS)
        local_total = group_total.reshape(query_count, HEADS)
        local_sum = group_sum.reshape(query_count, HEADS, head_dim)
        peer_top, peer_total, peer_sum = (
            lax.all_to_all(local_top[None], "qry", split_axis=1, concat_axis=0, tiled=True),
            lax.all_to_all(local_total[None], "qry", split_axis=1, concat_axis=0, tiled=True),
            lax.all_to_all(local_sum[None], "qry", split_axis=1, concat_axis=0, tiled=True),
        )
        owner_top = jnp.max(peer_top, axis=0)
        peer_factor = jnp.exp(peer_top - owner_top[None])
        owner_total = jnp.sum(peer_total * peer_factor, axis=0)
        owner_sum = jnp.sum(peer_sum * peer_factor[..., None], axis=0)
        merged_top, merged_total, merged_sum = merged(
            (owner_top, owner_total, owner_sum), "span", combine_parts
        )
        rows_here = state.shape[0]
        attn = (
            (merged_sum / merged_total[..., None]).reshape(rows_here, channels).astype(jnp.bfloat16)
        )
        state = state + jnp.dot(attn, w_out[layer_index], preferred_element_type=jnp.float32)
    query_embed = normalize(state, norm_gain)
    embed_all = lax.all_gather(query_embed, "qry", axis=0, tiled=True)
    mask_embed = jnp.dot(
        embed_all.astype(jnp.bfloat16), mask_weight, preferred_element_type=jnp.float32
    ).astype(jnp.bfloat16)
    logits = jnp.einsum(
        "nd,vd->nv", mask_embed, flat, preferred_element_type=jnp.float32
    ) * channels ** (-0.5)
    mask_logits = logits.astype(jnp.bfloat16).reshape(query_count, depth_cells, row_cells, x_cells)
    return (query_embed, mask_logits)


def solution(mesh):
    return jax.shard_map(
        local,
        mesh=mesh,
        in_specs=(
            P("span", "qry", None, None),
            P(),
            P("qry", None),
            P(),
            P(),
            P(),
            P(),
            P(),
            P(),
            P(),
        ),
        out_specs=(P("qry", None), P(None, "span", "qry", None)),
        check_vma=False,
    )
```

profile of v0, /device:TPU:0, one launch (start us, length us, event | category | flops | bytes accessed | tf_op | source)
XLA Modules:
  0.0 212.8 jit_solution(11684761800349429387)
XLA Ops:
  0.6 3.2 %collective-permute-start = (bf16[1,2,128,256]{3,2,1,0:T(8,128)(2,1)}, bf16[1,2,128,256]{3,2,1,0:T(8,128)(2,1)}, u32[]{:S(2)}, u32[]{:S(2)}) collective-permute-start(bf16[1,2,128,256]{3,2,1,0:T(8,128)(2,1)} %param.14), channel_id=1, source_target_pairs={{0,2},{2,4},{4,6},{6,8},{8,10},{10,12},{12,14},{14,16},{16,18},{18... | collective-permute-start | bytes 393224 | tf_op jit(solution)/shard_map/ppermute | solution.py:18
  7.0 2.0 fusion.59
  16.2 4.8 %all_gather.45 = bf16[16,256]{1,0:T(8,128)(2,1)S(1)} all-gather(bf16[8,256]{1,0:T(8,128)(2,1)S(1)} %convert.12), channel_id=1, replica_groups=mesh['span'=16,'qry'=2] {'qry'}, dimensions={0}, use_global_device_ids=true | all-gather | bytes 12288 | tf_op jit(solution)/shard_map/all_gather | solution.py:107
  30.5 4.0 %collective-permute-start.2 = (bf16[3,1,128,256]{3,2,1,0:T(8,128)(2,1)S(1)}, bf16[3,1,128,256]{3,2,1,0:T(8,128)(2,1)S(1)}, u32[]{:S(2)}, u32[]{:S(2)}) collective-permute-start(bf16[3,1,128,256]{3,2,1,0:T(8,128)(2,1)S(1)} %get-tuple-element.278), channel_id=1, source_target_pairs={{0,1},{2,3},{4,5},{6,7},{8,9},{10,11},{12,13},{14,15},{16,17},{18,... | collective-permute-start | bytes 589832 | tf_op jit(solution)/shard_map/ppermute | solution.py:18
  35.9 3.5 %collective-permute-done.2 = bf16[3,1,128,256]{3,2,1,0:T(8,128)(2,1)S(1)} collective-permute-done((bf16[3,1,128,256]{3,2,1,0:T(8,128)(2,1)S(1)}, bf16[3,1,128,256]{3,2,1,0:T(8,128)(2,1)S(1)}, u32[]{:S(2)}, u32[]{:S(2)}) %collective-permute-start.2) | collective-permute-done | bytes 196640 | tf_op jit(solution)/shard_map/ppermute | solution.py:18
  39.4 4.1 %collective-permute-done.3 = bf16[3,1,128,256]{3,2,1,0:T(8,128)(2,1)S(1)} collective-permute-done((bf16[3,1,128,256]{3,2,1,0:T(8,128)(2,1)S(1)}, bf16[3,1,128,256]{3,2,1,0:T(8,128)(2,1)S(1)}, u32[]{:S(2)}, u32[]{:S(2)}) %collective-permute-start.3) | collective-permute-done | bytes 196640 | tf_op jit(solution)/shard_map/ppermute | solution.py:20
  50.0 3.2 %all-to-all-start = ((f32[1,16,8]{2,0,1:T(1,128)}), f32[1,16,8]{2,0,1:T(1,128)S(1)}, u32[]{:S(2)}, u32[]{:S(2)}) async-start(f32[1,16,8]{2,0,1:T(1,128)} %copy.270), calls=%async_computation | async-start | bytes 16384 | tf_op jit(solution)/shard_map/all_to_all | solution.py:156
  54.8 2.2 %all-to-all-done = f32[1,16,8]{2,0,1:T(1,128)S(1)} async-done(((f32[1,16,8]{2,0,1:T(1,128)}), f32[1,16,8]{2,0,1:T(1,128)S(1)}, u32[]{:S(2)}, u32[]{:S(2)}) %all-to-all-start) | async-done | bytes 544 | tf_op jit(solution)/shard_map/all_to_all | solution.py:156
  57.0 3.2 %all-to-all-start.1 = ((f32[1,16,8]{2,0,1:T(1,128)}), f32[1,16,8]{2,0,1:T(1,128)S(1)}, u32[]{:S(2)}, u32[]{:S(2)}) async-start(f32[1,16,8]{2,0,1:T(1,128)} %copy.273), calls=%async_computation.1 | async-start | bytes 16384 | tf_op jit(solution)/shard_map/all_to_all | solution.py:157
  60.3 22.2 %all-gather = f32[128,8]{1,0:T(8,128)S(1)} all-gather(f32[8,8]{1,0:T(8,128)S(1)} %reduce_max.39), channel_id=2, replica_groups=mesh['span'=16,'qry'=2] {'span'}, dimensions={0}, use_global_device_ids=true | all-gather | bytes 4352 | tf_op jit(solution)/shard_map/all_gather | solution.py:28
  82.6 3.2 %all-to-all-start.2 = ((f32[2,1,2048]{2,1,0:T(1,128)}), f32[2,1,2048]{2,1,0:T(1,128)S(1)}, u32[]{:S(2)}, u32[]{:S(2)}) async-start(f32[2,1,2048]{2,1,0:T(1,128)} %reshape.391), calls=%async_computation.2 | async-start | bytes 32768 | tf_op jit(solution)/shard_map/all_to_all | solution.py:158
  86.1 17.7 %all-gather.1 = f32[128,8]{1,0:T(8,128)S(1)} all-gather(f32[8,8]{1,0:T(8,128)S(1)} %copy.275), channel_id=3, replica_groups=mesh['span'=16,'qry'=2] {'span'}, dimensions={0}, use_global_device_ids=true | all-gather | bytes 4352 | tf_op jit(solution)/shard_map/all_gather | solution.py:28
  105.2 20.3 %all-gather.2 = f32[128,8,32]{2,1,0:T(8,128)S(1)} all-gather(f32[8,8,32]{2,1,0:T(8,128)S(1)} %copy.278), channel_id=4, replica_groups=mesh['span'=16,'qry'=2] {'span'}, dimensions={0}, use_global_device_ids=true | all-gather | bytes 139264 | tf_op jit(solution)/shard_map/all_gather | solution.py:28
  125.5 2.0 while.4
  127.9 4.4 %all_gather.52 = bf16[16,256]{1,0:T(8,128)(2,1)S(1)} all-gather(bf16[8,256]{1,0:T(8,128)(2,1)S(1)} %get-tuple-element.282), channel_id=1, replica_groups=mesh['span'=16,'qry'=2] {'qry'}, dimensions={0}, use_global_device_ids=true | all-gather | bytes 12288 | tf_op jit(solution)/shard_map/all_gather | solution.py:107
  133.8 3.3 %all-to-all-start.3 = ((f32[1,16,8]{2,0,1:T(1,128)}), f32[1,16,8]{2,0,1:T(1,128)S(1)}, u32[]{:S(2)}, u32[]{:S(2)}) async-start(f32[1,16,8]{2,0,1:T(1,128)} %copy.284), calls=%async_computation.3 | async-start | bytes 16384 | tf_op jit(solution)/shard_map/all_to_all | solution.py:156
  138.5 2.4 %all-to-all-done.3 = f32[1,16,8]{2,0,1:T(1,128)S(1)} async-done(((f32[1,16,8]{2,0,1:T(1,128)}), f32[1,16,8]{2,0,1:T(1,128)S(1)}, u32[]{:S(2)}, u32[]{:S(2)}) %all-to-all-start.3) | async-done | bytes 544 | tf_op jit(solution)/shard_map/all_to_all | solution.py:156
  140.9 3.2 %all-to-all-start.4 = ((f32[1,16,8]{2,0,1:T(1,128)}), f32[1,16,8]{2,0,1:T(1,128)S(1)}, u32[]{:S(2)}, u32[]{:S(2)}) async-start(f32[1,16,8]{2,0,1:T(1,128)} %copy.287), calls=%async_computation.4 | async-start | bytes 16384 | tf_op jit(solution)/shard_map/all_to_all | solution.py:157
  144.1 17.5 %all-gather.3 = f32[128,8]{1,0:T(8,128)S(1)} all-gather(f32[8,8]{1,0:T(8,128)S(1)} %reduce_max.41), channel_id=5, replica_groups=mesh['span'=16,'qry'=2] {'span'}, dimensions={0}, use_global_device_ids=true | all-gather | bytes 4352 | tf_op jit(solution)/shard_map/all_gather | solution.py:28
  161.7 3.2 %all-to-all-start.5 = ((f32[2,1,2048]{2,1,0:T(1,128)}), f32[2,1,2048]{2,1,0:T(1,128)S(1)}, u32[]{:S(2)}, u32[]{:S(2)}) async-start(f32[2,1,2048]{2,1,0:T(1,128)} %reshape.393), calls=%async_computation.5 | async-start | bytes 32768 | tf_op jit(solution)/shard_map/all_to_all | solution.py:158
  165.2 19.2 %all-gather.4 = f32[128,8]{1,0:T(8,128)S(1)} all-gather(f32[8,8]{1,0:T(8,128)S(1)} %copy.289), channel_id=6, replica_groups=mesh['span'=16,'qry'=2] {'span'}, dimensions={0}, use_global_device_ids=true | all-gather | bytes 4352 | tf_op jit(solution)/shard_map/all_gather | solution.py:28
  185.3 18.9 %all-gather.5 = f32[128,8,32]{2,1,0:T(8,128)S(1)} all-gather(f32[8,8,32]{2,1,0:T(8,128)S(1)} %copy.292), channel_id=7, replica_groups=mesh['span'=16,'qry'=2] {'span'}, dimensions={0}, use_global_device_ids=true | all-gather | bytes 139264 | tf_op jit(solution)/shard_map/all_gather | solution.py:28
  204.2 2.0 while.5
  207.5 4.3 %all_gather.59 = bf16[16,256]{1,0:T(8,128)(2,1)S(1)} all-gather(bf16[8,256]{1,0:T(8,128)(2,1)S(1)} %get-tuple-element.234), channel_id=1, replica_groups=mesh['span'=16,'qry'=2] {'qry'}, dimensions={0}, use_global_device_ids=true | all-gather | bytes 12288 | tf_op jit(solution)/shard_map/all_gather | solution.py:173
  (229 shorter events, 40.3 us)
Async XLA Ops:
  0.6 211.2 %copy-start = (bf16[256,256]{1,0:T(8,128)(2,1)S(1)}, bf16[256,256]{1,0:T(8,128)(2,1)}, u32[]{:S(2)}) copy-start(bf16[256,256]{1,0:T(8,128)(2,1)} %param.22) | copy-start | bytes 393220
  0.6 28.0 %collective-permute-start = (bf16[1,2,128,256]{3,2,1,0:T(8,128)(2,1)}, bf16[1,2,128,256]{3,2,1,0:T(8,128)(2,1)}, u32[]{:S(2)}, u32[]{:S(2)}) collective-permute-start(bf16[1,2,128,256]{3,2,1,0:T(8,128)(2,1)} %param.14), channel_id=1, source_target_pairs={{0,2},{2,4},{4,6},{6,8},{8,10},{10,12},{12,14},{14,16},{16,18},{18... | collective-permute-start | bytes 393224 | tf_op jit(solution)/shard_map/ppermute | solution.py:18
  3.8 25.7 %collective-permute-start.1 = (bf16[1,2,128,256]{3,2,1,0:T(8,128)(2,1)}, bf16[1,2,128,256]{3,2,1,0:T(8,128)(2,1)}, u32[]{:S(2)}, u32[]{:S(2)}) collective-permute-start(bf16[1,2,128,256]{3,2,1,0:T(8,128)(2,1)} %param.14), channel_id=1, source_target_pairs={{2,0},{4,2},{6,4},{8,6},{10,8},{12,10},{14,12},{16,14},{18,16},{20... | collective-permute-start | bytes 393224 | tf_op jit(solution)/shard_map/ppermute | solution.py:20
  10.2 6.0 %copy-start.12 = (f32[8,256]{1,0:T(8,128)S(1)}, f32[8,256]{1,0:T(8,128)}, u32[]{:S(2)}) copy-start(f32[8,256]{1,0:T(8,128)} %param.16) | copy-start | bytes 24580
  10.3 11.7 %copy-start.1 = (bf16[1,1,1,256,256]{3,4,2,1,0:T(8,128)(2,1)S(1)}, bf16[1,1,1,256,256]{3,4,2,1,0:T(8,128)(2,1)}, u32[]{:S(2)}) copy-start(bf16[1,1,1,256,256]{3,4,2,1,0:T(8,128)(2,1)} %copy.332) | copy-start | bytes 393220
  11.6 10.5 %copy-start.2 = (bf16[1,1,1,256,256]{3,4,2,1,0:T(8,128)(2,1)S(1)}, bf16[1,1,1,256,256]{3,4,2,1,0:T(8,128)(2,1)}, u32[]{:S(2)}) copy-start(bf16[1,1,1,256,256]{3,4,2,1,0:T(8,128)(2,1)} %copy.338) | copy-start | bytes 393220
  16.2 6.0 %copy-start.3 = (bf16[1,1,1,256,256]{3,4,2,1,0:T(8,128)(2,1)S(1)}, bf16[1,1,1,256,256]{3,4,2,1,0:T(8,128)(2,1)}, u32[]{:S(2)}) copy-start(bf16[1,1,1,256,256]{3,4,2,1,0:T(8,128)(2,1)} %copy.329) | copy-start | bytes 393220
  22.0 1.2 copy-start.4
  22.1 1.2 copy-start.5
  22.1 1.2 copy-start.6
  26.9 2.6 %copy-start.11 = (bf16[1,2,128,256]{3,2,1,0:T(8,128)(2,1)S(1)}, bf16[1,2,128,256]{3,2,1,0:T(8,128)(2,1)}, u32[]{:S(2)}) copy-start(bf16[1,2,128,256]{3,2,1,0:T(8,128)(2,1)} %param.14) | copy-start | bytes 393220
  30.5 8.9 %collective-permute-start.2 = (bf16[3,1,128,256]{3,2,1,0:T(8,128)(2,1)S(1)}, bf16[3,1,128,256]{3,2,1,0:T(8,128)(2,1)S(1)}, u32[]{:S(2)}, u32[]{:S(2)}) collective-permute-start(bf16[3,1,128,256]{3,2,1,0:T(8,128)(2,1)S(1)} %get-tuple-element.278), channel_id=1, source_target_pairs={{0,1},{2,3},{4,5},{6,7},{8,9},{10,11},{12,13},{14,15},{16,17},{18,... | collective-permute-start | bytes 589832 | tf_op jit(solution)/shard_map/ppermute | solution.py:18
  34.5 9.0 %collective-permute-start.3 = (bf16[3,1,128,256]{3,2,1,0:T(8,128)(2,1)S(1)}, bf16[3,1,128,256]{3,2,1,0:T(8,128)(2,1)S(1)}, u32[]{:S(2)}, u32[]{:S(2)}) collective-permute-start(bf16[3,1,128,256]{3,2,1,0:T(8,128)(2,1)S(1)} %get-tuple-element.279), channel_id=1, source_target_pairs={{1,0},{3,2},{5,4},{7,6},{9,8},{11,10},{13,12},{15,14},{17,16},{19,... | collective-permute-start | bytes 589832 | tf_op jit(solution)/shard_map/ppermute | solution.py:20
  46.8 1.4 copy-start.8
  50.0 7.0 %all-to-all-start = ((f32[1,16,8]{2,0,1:T(1,128)}), f32[1,16,8]{2,0,1:T(1,128)S(1)}, u32[]{:S(2)}, u32[]{:S(2)}) async-start(f32[1,16,8]{2,0,1:T(1,128)} %copy.270), calls=%async_computation | async-start | bytes 16384 | tf_op jit(solution)/shard_map/all_to_all | solution.py:156
  57.0 25.6 %all-to-all-start.1 = ((f32[1,16,8]{2,0,1:T(1,128)}), f32[1,16,8]{2,0,1:T(1,128)S(1)}, u32[]{:S(2)}, u32[]{:S(2)}) async-start(f32[1,16,8]{2,0,1:T(1,128)} %copy.273), calls=%async_computation.1 | async-start | bytes 16384 | tf_op jit(solution)/shard_map/all_to_all | solution.py:157
  82.5 45.2 %copy-start.10 = (bf16[2,256,256]{2,1,0:T(8,128)(2,1)S(1)}, bf16[2,256,256]{2,1,0:T(8,128)(2,1)}, u32[]{:S(2)}) copy-start(bf16[2,256,256]{2,1,0:T(8,128)(2,1)} %param.20) | copy-start | bytes 786436
  82.5 45.2 %copy-start.13 = (f32[8,256]{1,0:T(8,128)S(1)}, f32[8,256]{1,0:T(8,128)}, u32[]{:S(2)}) copy-start(f32[8,256]{1,0:T(8,128)} %param.16) | copy-start | bytes 24580
  82.6 21.2 %all-to-all-start.2 = ((f32[2,1,2048]{2,1,0:T(1,128)}), f32[2,1,2048]{2,1,0:T(1,128)S(1)}, u32[]{:S(2)}, u32[]{:S(2)}) async-start(f32[2,1,2048]{2,1,0:T(1,128)} %reshape.391), calls=%async_computation.2 | async-start | bytes 32768 | tf_op jit(solution)/shard_map/all_to_all | solution.py:158
  86.1 46.1 %copy-start.9 = (bf16[2,256,256]{2,1,0:T(8,128)(2,1)S(1)}, bf16[2,256,256]{2,1,0:T(8,128)(2,1)}, u32[]{:S(2)}) copy-start(bf16[2,256,256]{2,1,0:T(8,128)(2,1)} %param.17) | copy-start | bytes 786436
  133.8 7.1 %all-to-all-start.3 = ((f32[1,16,8]{2,0,1:T(1,128)}), f32[1,16,8]{2,0,1:T(1,128)S(1)}, u32[]{:S(2)}, u32[]{:S(2)}) async-start(f32[1,16,8]{2,0,1:T(1,128)} %copy.284), calls=%async_computation.3 | async-start | bytes 16384 | tf_op jit(solution)/shard_map/all_to_all | solution.py:156
  140.9 20.9 %all-to-all-start.4 = ((f32[1,16,8]{2,0,1:T(1,128)}), f32[1,16,8]{2,0,1:T(1,128)S(1)}, u32[]{:S(2)}, u32[]{:S(2)}) async-start(f32[1,16,8]{2,0,1:T(1,128)} %copy.287), calls=%async_computation.4 | async-start | bytes 16384 | tf_op jit(solution)/shard_map/all_to_all | solution.py:157
  161.7 22.7 %all-to-all-start.5 = ((f32[2,1,2048]{2,1,0:T(1,128)}), f32[2,1,2048]{2,1,0:T(1,128)S(1)}, u32[]{:S(2)}, u32[]{:S(2)}) async-start(f32[2,1,2048]{2,1,0:T(1,128)} %reshape.393), calls=%async_computation.5 | async-start | bytes 32768 | tf_op jit(solution)/shard_map/all_to_all | solution.py:158
  165.2 41.7 %copy-start.15 = (f32[256]{0:T(256)S(1)}, f32[256]{0:T(256)}, u32[]{:S(2)}) copy-start(f32[256]{0:T(256)} %param.21) | copy-start | bytes 3076
  (2 other events, 2.2 us)
where the time goes:
time: 214 us; the launch traced here: 213 us
  blocking collectives  129 us (60%)
  starting transfers between devices  29.2 us (14%)
  local copies, waits for them, and re-layouts  24 us (11%)
  waiting for transfers between devices  12.3 us (6%)
  other arithmetic  9.45 us (4%)
  matrix products  6.3 us (3%)
    all_gather x6, blocking collectives, merged(): pieces = jax.tree.map(lambda part: lax.all_gather(part, axis), value)  116 us
    unnamed x68, local copies, waits for them, and re-layouts  13.9 us
    all_gather x2, blocking collectives, local(): state_all = lax.all_gather(state, 'qry', axis=0, tiled=True)  9.14 us
    ppermute x2, starting transfers between devices, with_halo(): lax.ppermute(tail, axis, [(i, (i + 1) % count) for i in range(ends)])  7.15 us
    all_to_all x2, starting transfers between devices, local(): lax.all_to_all(local_top[None], 'qry', split_axis=1, concat_axis=0, tiled...  6.52 us
    all_to_all x2, starting transfers between devices, local(): lax.all_to_all(local_sum[None], 'qry', split_axis=1, concat_axis=0, tiled...  6.5 us
    all_to_all x2, starting transfers between devices, local(): lax.all_to_all(local_total[None], 'qry', split_axis=1, concat_axis=0, til...  6.45 us
    all_to_all x2, waiting for transfers between devices, local(): lax.all_to_all(local_top[None], 'qry', split_axis=1, concat_axis=0, tiled...  4.64 us
  transfers between devices with their start and end apart: 10, of which 4 were waited for; matrix products, arithmetic and copies ran while one was open for 11% of the time, Pallas kernels for 0%

commit v1 on v0

v1 whole, which is shorter than its diff:
```python
import functools

import jax
import jax.numpy as jnp
from jax import lax
from jax.experimental import pallas as pl
from jax.experimental.pallas import tpu as pltpu
from jax.sharding import PartitionSpec as P

HEADS = 8
LAYERS = 2
LANES = 128
SLOTS = 8
F32 = jnp.float32
BF16 = jnp.bfloat16
EXACT = lax.Precision.HIGHEST


def iota(shape, dim):
    return lax.broadcasted_iota(jnp.int32, shape, dim)


def swap_partner(index, count, parity):
    other = index ^ 1 if parity == 0 else ((index + 1) ^ 1) - 1
    return other if 0 <= other < count else None


def swap(value, axes, counts, parities):
    pairs = []
    for first in range(counts[0]):
        for second in range(counts[1]):
            ends = [
                index if parity is None else swap_partner(index, count, parity)
                for index, count, parity in zip((first, second), counts, parities)
            ]
            if None not in ends:
                pairs.append((first * counts[1] + second, ends[0] * counts[1] + ends[1]))
    return lax.ppermute(value, axes, pairs)


def partials(qproj, keys, values, mask_rows, base, x_cells, out_ref):
    voxels, channels = keys.shape
    query_count = qproj.shape[0]
    blocks = voxels // x_cells
    rows = blocks * HEADS
    head_dim = channels // HEADS
    block_of_row = base + iota((rows, query_count), 0) // HEADS
    listed = mask_rows[0:1, :] == block_of_row
    for place in range(1, mask_rows.shape[0]):
        listed = listed | (mask_rows[place : place + 1, :] == block_of_row)
    chosen = jnp.dot(listed.astype(F32).astype(BF16), qproj, preferred_element_type=F32)
    own_head = iota((rows, channels), 1) // head_dim == iota((rows, channels), 0) % HEADS
    chosen = jnp.where(own_head, chosen, 0.0).astype(BF16)
    scores = lax.dot_general(chosen, keys, (((1,), (1,)), ((), ())), preferred_element_type=F32)
    allowed = iota((rows, voxels), 1) // x_cells == iota((rows, voxels), 0) // HEADS
    top = jnp.max(jnp.where(allowed, scores, -jnp.inf), axis=1, keepdims=True)
    prob = jnp.where(allowed, jnp.exp(scores - top), 0.0)
    total = jnp.sum(prob, axis=1, keepdims=True)
    weighted = jnp.dot(prob.astype(BF16), values, preferred_element_type=F32)
    weighted = jnp.where(own_head, weighted, 0.0)
    lane_head = iota((rows, LANES), 1) == iota((rows, LANES), 0) % HEADS
    top = jnp.where(lane_head, top, 0.0)
    total = jnp.where(lane_head, total, 0.0)
    wide = channels // LANES
    for block in range(blocks):
        span = slice(block * HEADS, (block + 1) * HEADS)
        summed = jnp.sum(weighted[span], axis=0, keepdims=True)
        for part in range(wide):
            row = block * wide + part
            out_ref[row : row + 1, :] = summed[:, part * LANES : (part + 1) * LANES]
        row = blocks * wide + block
        out_ref[row : row + 1, :] = jnp.sum(top[span], axis=0, keepdims=True)
        row = blocks * (wide + 1) + block
        out_ref[row : row + 1, :] = jnp.sum(total[span], axis=0, keepdims=True)


def merged(parts_ref, mask_column, blocks, channels, query_count):
    wide = channels // LANES
    slots = blocks * (wide + 2)
    devices = parts_ref.shape[0] // slots
    listed = mask_column.shape[0]
    places = listed // query_count

    def slot(index):
        return parts_ref[pl.ds(index, devices, stride=slots), :]

    by_block = jnp.concatenate(
        [
            jnp.concatenate(
                [slot(block * wide + part) for part in range(wide)]
                + [slot(blocks * wide + block), slot(blocks * (wide + 1) + block)],
                axis=1,
            )
            for block in range(blocks)
        ],
        axis=0,
    )
    column = iota((listed, devices * blocks), 1)
    block_id = (column % devices) * blocks + column // devices
    pick = (mask_column == block_id).astype(F32)
    picked = jnp.dot(pick, by_block, precision=EXACT, preferred_element_type=F32)

    def place(index, start, size):
        return picked[index * query_count : (index + 1) * query_count, start : start + size]

    tops = [place(index, channels, LANES) for index in range(places)]
    totals = [place(index, channels + LANES, LANES) for index in range(places)]
    top = functools.reduce(jnp.maximum, tops)
    factors = [jnp.exp(part - top) for part in tops]
    total = sum(factor * part for factor, part in zip(factors, totals))
    valid = iota((query_count, LANES), 1) < HEADS
    shares = [jnp.where(valid, factor / total, 0.0) for factor in factors]
    spread = (
        iota((LANES, channels), 1) // (channels // HEADS) == iota((LANES, channels), 0)
    ).astype(F32)
    wide_shares = jnp.dot(
        jnp.concatenate(shares, axis=0), spread, precision=EXACT, preferred_element_type=F32
    )
    attn = sum(
        wide_shares[index * query_count : (index + 1) * query_count] * place(index, 0, channels)
        for index in range(places)
    )
    return attn.astype(BF16)


def project(state, w_query, head_dim):
    return (
        jnp.dot(state.astype(BF16), w_query, preferred_element_type=F32) * head_dim ** (-0.5)
    ).astype(BF16)


def conv_kernel(rows_out, *refs):
    (own, plane_even, plane_odd, *rest) = refs
    halos = rest[: 3 * rows_out]
    (taps_hbm, queries, peers, w_query, w_key, w_value, mask_rows) = rest[
        3 * rows_out : 3 * rows_out + 7
    ]
    (pixel, states, parts, cells, taps, arrived) = rest[3 * rows_out + 7 :]
    row_cells, x_cells, channels = own.shape
    depth_id = lax.axis_index("span")
    row_id = lax.axis_index("qry")
    copies = []
    for depth_off in range(3):
        chunk = pl.ds(9 * depth_off, 9)
        copies.append(
            pltpu.make_async_copy(taps_hbm.at[chunk], taps.at[chunk], arrived.at[depth_off])
        )
        copies[-1].start()
    odd = depth_id % 2
    even_plane = 2 - 2 * odd
    odd_plane = 2 * odd
    blank = jnp.zeros((x_cells, channels), BF16)
    for depth_off in range(3):
        cells[depth_off, 0] = blank
        cells[depth_off, row_cells + 1] = blank
    for row in range(row_cells):
        cells[1, row + 1] = own[row]
        cells[even_plane, row + 1] = plane_even[row]
        cells[odd_plane, row + 1] = plane_odd[row]
    low = row_id % 2 == 0
    for parity in range(rows_out):
        at_end = low if parity == 0 else jnp.logical_not(low)
        row = jnp.where(at_end, row_cells + 1, 0)
        cells[1, row] = halos[3 * parity][...]
        cells[even_plane, row] = halos[3 * parity + 1][...]
        cells[odd_plane, row] = halos[3 * parity + 2][...]
    voxels = row_cells * x_cells
    sums = [None, None, None]
    for depth_off in range(3):
        copies[depth_off].wait()
        for row_off in range(3):
            slab = cells[depth_off, row_off : row_off + row_cells].reshape(voxels, channels)
            for x_off in range(3):
                product = jnp.dot(
                    slab, taps[9 * depth_off + 3 * row_off + x_off], preferred_element_type=F32
                )
                sums[x_off] = product if sums[x_off] is None else sums[x_off] + product
    x_id = iota((voxels, channels), 0) % x_cells
    conv = (
        sums[1]
        + jnp.where(x_id == 0, 0.0, pltpu.roll(sums[0], 1, 0))
        + jnp.where(x_id == x_cells - 1, 0.0, pltpu.roll(sums[2], voxels - 1, 0))
    )
    flat = jnp.maximum(conv, 0.0).astype(BF16)
    pixel[...] = flat
    here = queries.shape[0]
    if peers.shape[0] == states.shape[0]:
        states[...] = peers[...]
    else:
        states[pl.ds(pl.multiple_of(row_id * here, here), here), :] = queries[...]
        states[pl.ds(pl.multiple_of((1 - row_id) * here, here), here), :] = peers[...]
    qproj = project(states[...], w_query[0], channels // HEADS)
    keys = jnp.dot(flat, w_key[0], preferred_element_type=F32).astype(BF16)
    values = jnp.dot(flat, w_value[0], preferred_element_type=F32).astype(BF16)
    base = (depth_id * lax.axis_size("qry") + row_id) * row_cells
    partials(qproj, keys, values, mask_rows[...], base, x_cells, parts)


def layer_kernel(
    layer,
    x_cells,
    pixel,
    states,
    gathered,
    w_out,
    w_query,
    w_key,
    w_value,
    mask_rows,
    mask_column,
    new_states,
    parts,
):
    voxels, channels = pixel.shape
    blocks = voxels // x_cells
    flat = pixel[...]
    keys = jnp.dot(flat, w_key[layer], preferred_element_type=F32).astype(BF16)
    values = jnp.dot(flat, w_value[layer], preferred_element_type=F32).astype(BF16)
    attn = merged(gathered, mask_column[...], blocks, channels, states.shape[0])
    state = states[...] + jnp.dot(attn, w_out[layer - 1], preferred_element_type=F32)
    new_states[...] = state
    qproj = project(state, w_query[layer], channels // HEADS)
    base = (lax.axis_index("span") * lax.axis_size("qry") + lax.axis_index("qry")) * blocks
    partials(qproj, keys, values, mask_rows[...], base, x_cells, parts)


def final_kernel(
    x_cells, pixel, states, gathered, w_out, norm_gain, mask_weight, mask_column, embed, logits, all_rows
):
    voxels, channels = pixel.shape
    blocks = voxels // x_cells
    attn = merged(gathered, mask_column[...], blocks, channels, states.shape[0])
    state = states[...] + jnp.dot(attn, w_out[LAYERS - 1], preferred_element_type=F32)
    mean = jnp.mean(state, axis=-1, keepdims=True)
    centered = state - mean
    var = jnp.mean(centered * centered, axis=-1, keepdims=True)
    query_embed = centered * lax.rsqrt(var + 1e-05) * norm_gain[...]
    all_rows[...] = query_embed
    here = embed.shape[0]
    embed[...] = all_rows[pl.ds(pl.multiple_of(lax.axis_index("qry") * here, here), here), :]
    mask_embed = jnp.dot(
        query_embed.astype(BF16), mask_weight[...], preferred_element_type=F32
    ).astype(BF16)
    scores = lax.dot_general(
        mask_embed, pixel[...], (((1,), (1,)), ((), ())), preferred_element_type=F32
    ) * channels ** (-0.5)
    for block in range(blocks):
        logits[:, block, :] = scores[:, block * x_cells : (block + 1) * x_cells].astype(BF16)


def shape(dims, dtype):
    return jax.ShapeDtypeStruct(dims, dtype)


VMEM = pl.BlockSpec(memory_space=pltpu.VMEM)
ANY = pl.BlockSpec(memory_space=pl.ANY)


def exchange(parts, devices):
    axes = ("span", "qry")
    copies = jnp.broadcast_to(parts[None], (devices, *parts.shape))
    gathered = lax.all_to_all(copies, axes, split_axis=0, concat_axis=0, tiled=True)
    return gathered.reshape(devices * parts.shape[0], LANES)


def local(
    counts,
    features,
    conv_weight,
    queries,
    w_query,
    w_key,
    w_value,
    w_out,
    norm_gain,
    mask_weight,
    mask_blocks,
):
    depth_cells, row_cells, x_cells, channels = features.shape
    assert depth_cells == 1
    axes = ("span", "qry")
    devices = counts[0] * counts[1]
    query_count, places = mask_blocks.shape
    voxels = row_cells * x_cells
    slots = row_cells * (channels // LANES + 2)
    own = features[0]
    plane_odd = swap(own, axes, counts, (1, None))
    plane_even = swap(own, axes, counts, (0, None))
    row_low = lax.axis_index("qry") % 2 == 0
    halos = []
    parities = (0,) if counts[1] == 2 else (0, 1)
    for parity in parities:
        at_end = row_low if parity == 0 else jnp.logical_not(row_low)
        edge = lax.dynamic_index_in_dim(
            own, jnp.where(at_end, row_cells - 1, 0), axis=0, keepdims=False
        )
        row = swap(edge, axes, counts, (None, parity))
        corner_odd = swap(edge, axes, counts, (1, parity))
        corner_even = swap(row, axes, counts, (0, None))
        halos += [row, corner_even, corner_odd]
    if counts[1] == 2:
        peers = swap(queries, axes, counts, (None, 0))
    else:
        peers = lax.all_gather(queries, "qry", axis=0, tiled=True)
    mask_rows = mask_blocks.T
    mask_column = mask_rows.reshape(places * query_count, 1)
    pixel, states, parts = pl.pallas_call(
        functools.partial(conv_kernel, len(parities)),
        out_shape=(
            shape((voxels, channels), BF16),
            shape((query_count, channels), F32),
            shape((slots, LANES), F32),
        ),
        in_specs=[VMEM] * (3 + len(halos)) + [ANY] + [VMEM] * 6,
        out_specs=[VMEM] * 3,
        scratch_shapes=[
            pltpu.VMEM((3, row_cells + 2, x_cells, channels), BF16),
            pltpu.VMEM(conv_weight.shape, BF16),
            pltpu.SemaphoreType.DMA((3,)),
        ],
        name="conv_partials",
    )(
        own,
        plane_even,
        plane_odd,
        *halos,
        conv_weight,
        queries,
        peers,
        w_query,
        w_key,
        w_value,
        mask_rows,
    )
    for layer in range(1, LAYERS):
        states, parts = pl.pallas_call(
            functools.partial(layer_kernel, layer, x_cells),
            out_shape=(shape((query_count, channels), F32), shape((slots, LANES), F32)),
            in_specs=[VMEM] * 9,
            out_specs=[VMEM] * 2,
            name="layer_partials",
        )(
            pixel,
            states,
            exchange(parts, devices),
            w_out,
            w_query,
            w_key,
            w_value,
            mask_rows,
            mask_column,
        )
    embed, logits = pl.pallas_call(
        functools.partial(final_kernel, x_cells),
        out_shape=(
            shape(queries.shape, F32),
            shape((query_count, row_cells, x_cells), BF16),
        ),
        in_specs=[VMEM] * 7,
        out_specs=[VMEM] * 2,
        scratch_shapes=[pltpu.VMEM((query_count, channels), F32)],
        name="final_logits",
    )(
        pixel,
        states,
        exchange(parts, devices),
        w_out,
        norm_gain.reshape(1, channels),
        mask_weight,
        mask_column,
    )
    return embed, logits.reshape(query_count, depth_cells, row_cells, x_cells)


def solution(mesh):
    counts = (mesh.shape["span"], mesh.shape["qry"])
    return jax.shard_map(
        functools.partial(local, counts),
        mesh=mesh,
        in_specs=(
            P("span", "qry", None, None),
            P(),
            P("qry", None),
            P(),
            P(),
            P(),
            P(),
            P(),
            P(),
            P(),
        ),
        out_specs=(P("qry", None), P(None, "span", "qry", None)),
        check_vma=False,
    )
```

time: 214 us -> 54.9 us (0.26)
  blocking collectives: 129 us -> 11 us
  local copies, waits for them, and re-layouts: 24 us -> 4.93 us
  starting transfers between devices: 29.2 us -> 15.9 us
  Pallas kernels: 0 us -> 11.2 us
  other arithmetic: 9.45 us -> 0 us
  matrix products: 6.3 us -> 0 us
    all_gather x9 -> x0, blocking collectives: 129 us -> none  [the longest x6 116 us: merged(): pieces = jax.tree.map(lambda part: lax.all_gather(part, axis), value)]
    all_to_all x6 -> x1, starting transfers between devices: 19.5 us -> 6.24 us  [exchange(): lax.all_to_all(copies, axes, split_axis=0, concat_axis=0, tiled=True)]
    unnamed x68 -> x16, local copies, waits for them, and re-layouts: 13.9 us -> 1.33 us
    pallas_call x0 -> x3, Pallas kernels: none -> 11.2 us  [the longest x1 5.24 us: local(): pl.pallas_call(functools.partial(conv_kernel, len(parities)), out_shape=(...]
    all_to_all x0 -> x1, blocking collectives: none -> 11 us  [exchange(): lax.all_to_all(copies, axes, split_axis=0, concat_axis=0, tiled=True)]
    dot_general x22 -> x0, matrix products: 6.3 us -> none  [the longest x9 2.75 us: local(): product = jnp.dot(slab, wide_taps, preferred_element_type=jnp.float32)]
    ppermute x4 -> x6, waiting for transfers between devices: 7.67 us -> 2.75 us  [swap(): return lax.ppermute(value, axes, pairs)]
    slice x18 -> x0, local copies, waits for them, and re-layouts: 4.26 us -> none  [the longest x1 2 us: local(): taps[depth_off, row_off, 1]]
  transfers between devices with their start and end apart: 10 -> 7, of which waited for: 4 -> 3; matrix products, arithmetic and copies ran while one was open for 11% -> 1% of each run, Pallas kernels for 0% -> 0%
where the time goes in v1:
time: 54.9 us; the launch traced here: 54.5 us
  starting transfers between devices  15.9 us (29%)
  Pallas kernels  11.2 us (20%)
  blocking collectives  11 us (20%)
  waiting for transfers between devices  10.6 us (19%)
  local copies, waits for them, and re-layouts  4.93 us (9%)
  between operations  0.76 us (1%)
    all_to_all x1, blocking collectives, exchange(): lax.all_to_all(copies, axes, split_axis=0, concat_axis=0, tiled=True)  11 us
    ppermute x6, starting transfers between devices, swap(): return lax.ppermute(value, axes, pairs)  9.7 us
    all_to_all x1, waiting for transfers between devices, exchange(): lax.all_to_all(copies, axes, split_axis=0, concat_axis=0, tiled=True)  7.88 us
    all_to_all x1, starting transfers between devices, exchange(): lax.all_to_all(copies, axes, split_axis=0, concat_axis=0, tiled=True)  6.24 us
    pallas_call x1, Pallas kernels, local(): pl.pallas_call(functools.partial(conv_kernel, len(parities)), out_shape=(...  5.24 us
    pallas_call x1, Pallas kernels, local(): pl.pallas_call(functools.partial(layer_kernel, layer, x_cells), out_shape...  3.15 us
    pallas_call x1, Pallas kernels, local(): pl.pallas_call(functools.partial(final_kernel, x_cells), out_shape=(shape...  2.83 us
    ppermute x6, waiting for transfers between devices, swap(): return lax.ppermute(value, axes, pairs)  2.75 us
  transfers between devices with their start and end apart: 7, of which 3 were waited for; matrix products, arithmetic and copies ran while one was open for 1% of the time, Pallas kernels for 0%

profile of v1, /device:TPU:0, one launch (start us, length us, event | category | flops | bytes accessed | tf_op | source)
XLA Modules:
  0.0 54.5 jit_solution(16716967636780316372)
XLA Ops:
  0.6 0.0 copy-start.6
  0.7 0.8 %dynamic-slice_bitcast_fusion = bf16[128,256]{1,0:T(8,128)(2,1)S(1)} fusion(bf16[1,2,128,256]{3,2,1,0:T(8,128)(2,1)} %param.10, s32[]{:T(128)S(6)} %select_n.14), kind=kLoop, calls=%fused_computation | loop fusion | bytes 131076 | tf_op jit(solution)/shard_map/jit(dynamic_index_in_dim)/squeeze | solution.py:294
  1.5 3.0 %collective-permute-start.2 = (bf16[128,256]{1,0:T(8,128)(2,1)S(1)}, bf16[128,256]{1,0:T(8,128)(2,1)S(1)}, u32[]{:S(2)}, u32[]{:S(2)}) collective-permute-start(bf16[128,256]{1,0:T(8,128)(2,1)S(1)} %dynamic-slice_bitcast_fusion), channel_id=1, source_target_pairs={{0,1},{1,0},{2,3},{3,2},{4,5},{5,4},{6,7},{7,6},{8,9},{9,8},{10,11... | collective-permute-start | bytes 196616 | tf_op jit(solution)/shard_map/ppermute | solution.py:38
  4.5 0.7 %collective-permute-start.1 = (bf16[2,128,256]{2,1,0:T(8,128)(2,1)}, bf16[2,128,256]{2,1,0:T(8,128)(2,1)S(1)}, u32[]{:S(2)}, u32[]{:S(2)}) collective-permute-start(bf16[2,128,256]{2,1,0:T(8,128)(2,1)} %bitcast.13), channel_id=1, source_target_pairs={{2,4},{3,5},{4,2},{5,3},{6,8},{7,9},{8,6},{9,7},{10,12},{11,13},{1... | collective-permute-start | bytes 393224 | tf_op jit(solution)/shard_map/ppermute | solution.py:38
  5.2 0.7 %collective-permute-start.4 = (bf16[128,256]{1,0:T(8,128)(2,1)S(1)}, bf16[128,256]{1,0:T(8,128)(2,1)S(1)}, u32[]{:S(2)}, u32[]{:S(2)}) collective-permute-start(bf16[128,256]{1,0:T(8,128)(2,1)S(1)} %dynamic-slice_bitcast_fusion), channel_id=1, source_target_pairs={{2,5},{3,4},{4,3},{5,2},{6,9},{7,8},{8,7},{9,6},{10,13},{11,12},{1... | collective-permute-start | bytes 196616 | tf_op jit(solution)/shard_map/ppermute | solution.py:38
  5.8 0.9 %collective-permute-done.2.refs_3_ = bf16[128,256]{1,0:T(8,128)(2,1)S(1)} collective-permute-done((bf16[128,256]{1,0:T(8,128)(2,1)S(1)}, bf16[128,256]{1,0:T(8,128)(2,1)S(1)}, u32[]{:S(2)}, u32[]{:S(2)}) %collective-permute-start.2) | collective-permute-done | bytes 65568 | tf_op jit(solution)/shard_map/ppermute | solution.py:38
  6.7 3.4 %collective-permute-start.3 = (bf16[128,256]{1,0:T(8,128)(2,1)S(1)}, bf16[128,256]{1,0:T(8,128)(2,1)S(1)}, u32[]{:S(2)}, u32[]{:S(2)}) collective-permute-start(bf16[128,256]{1,0:T(8,128)(2,1)S(1)} %collective-permute-done.2.refs_3_), channel_id=1, source_target_pairs={{0,2},{1,3},{2,0},{3,1},{4,6},{5,7},{6,4},{7,5},{8,10},{9,11},{10,... | collective-permute-start | bytes 196616 | tf_op jit(solution)/shard_map/ppermute | solution.py:38
  10.1 2.0 %collective-permute-start.5 = (f32[8,256]{1,0:T(8,128)}, f32[8,256]{1,0:T(8,128)S(1)}, u32[]{:S(2)}, u32[]{:S(2)}) collective-permute-start(f32[8,256]{1,0:T(8,128)} %refs_7_.1), channel_id=1, source_target_pairs={{0,1},{1,0},{2,3},{3,2},{4,5},{5,4},{6,7},{7,6},{8,9},{9,8},{10,11... | collective-permute-start | bytes 24584 | tf_op jit(solution)/shard_map/ppermute | solution.py:38
  12.1 1.8 %collective-permute-done.5.refs_8_ = f32[8,256]{1,0:T(8,128)S(1)} collective-permute-done((f32[8,256]{1,0:T(8,128)}, f32[8,256]{1,0:T(8,128)S(1)}, u32[]{:S(2)}, u32[]{:S(2)}) %collective-permute-start.5) | collective-permute-done | bytes 8224 | tf_op jit(solution)/shard_map/ppermute | solution.py:38
  14.0 0.5 copy-done.7
  14.6 0.0 copy-done.4
  14.6 0.0 copy-done.5
  14.6 0.1 copy-done.1
  14.7 0.0 copy-done.2
  14.7 5.2 %conv_partials.1 = (bf16[256,256]{1,0:T(8,128)(2,1)}, f32[16,256]{1,0:T(8,128)}, f32[8,128]{1,0:T(8,128)}) custom-call(bf16[2,128,256]{2,1,0:T(8,128)(2,1)} %bitcast.14, bf16[2,128,256]{2,1,0:T(8,128)(2,1)} %copy-done.1, bf16[2,128,256]{2,1,0:T(8,128)(2,1)} %copy-done.2, bf16[128,256]{1,0:T(8,128)(2,1)} %copy-done.3, bf16[128,256]{1,0:T(8,128)(2,1)} %copy-done.5, ...), custom_call_target="tpu_custom_call" | custom-call | tf_op jit(solution)/shard_map/conv_partials/pallas_call | solution.py:307
  19.9 1.4 %broadcast_in_dim.4 = f32[32,8,128]{2,1,0:T(8,128)} broadcast(f32[8,128]{1,0:T(8,128)} %get-tuple-element.11), dimensions={1,2} | broadcast | bytes 135168 | tf_op jit(solution)/shard_map/broadcast_in_dim | solution.py:261
  21.3 6.2 %all-to-all-start = ((f32[32,8,128]{2,1,0:T(8,128)}), f32[32,8,128]{2,1,0:T(8,128)S(1)}, u32[]{:S(2)}, u32[]{:S(2)}) async-start(f32[32,8,128]{2,1,0:T(8,128)} %broadcast_in_dim.4), calls=%async_computation | async-start | bytes 262144 | tf_op jit(solution)/shard_map/all_to_all | solution.py:262
  27.6 0.7 %reshape.28.mask_column = s32[64,1]{1,0:T(8,128)} reshape(s32[4,16]{1,0:T(4,128)S(1)} %bitcast.17) | data formatting | bytes 512 | tf_op jit(solution)/shard_map/reshape | solution.py:306
  28.3 7.9 %all-to-all-done = f32[32,8,128]{2,1,0:T(8,128)S(1)} async-done(((f32[32,8,128]{2,1,0:T(8,128)}), f32[32,8,128]{2,1,0:T(8,128)S(1)}, u32[]{:S(2)}, u32[]{:S(2)}) %all-to-all-start) | async-done | bytes 131104 | tf_op jit(solution)/shard_map/all_to_all | solution.py:262
  36.2 0.7 %copy-done = f32[32,8,128]{2,1,0:T(8,128)} copy-done((f32[32,8,128]{2,1,0:T(8,128)}, f32[32,8,128]{2,1,0:T(8,128)S(1)}, u32[]{:S(2)}) %copy-start) | copy-done | bytes 131096
  36.8 3.1 %layer_partials.1 = (f32[16,256]{1,0:T(8,128)}, f32[8,128]{1,0:T(8,128)}) custom-call(bf16[256,256]{1,0:T(8,128)(2,1)} %get-tuple-element.9.pixel, f32[16,256]{1,0:T(8,128)} %get-tuple-element.10.states, f32[256,128]{1,0:T(8,128)} %bitcast.11, bf16[2,256,256]{2,1,0:T(8,128)(2,1)} %w_out.3, bf16[2,256,256]{2,1,0:T(8,128)(2,1)} %w_query.1, ...), custom_call_target="tpu_custom_call" | custom-call | tf_op jit(solution)/shard_map/layer_partials/pallas_call | solution.py:336
  40.0 0.7 %broadcast_in_dim.5 = f32[32,8,128]{2,1,0:T(8,128)S(1)} broadcast(f32[8,128]{1,0:T(8,128)} %get-tuple-element.13), dimensions={1,2} | broadcast | bytes 135168 | tf_op jit(solution)/shard_map/broadcast_in_dim | solution.py:261
  40.7 11.0 %all_to_all.10 = f32[32,8,128]{2,1,0:T(8,128)} all-to-all(f32[32,8,128]{2,1,0:T(8,128)S(1)} %broadcast_in_dim.5), channel_id=1, replica_groups=mesh['span'=16,'qry'=2] {'span','qry'}, dimensions={0} | all-to-all | bytes 262144 | tf_op jit(solution)/shard_map/all_to_all | solution.py:262
  51.6 2.8 %final_logits.1 = (f32[8,256]{1,0:T(8,128)}, bf16[16,2,128]{2,1,0:T(2,128)(2,1)}) custom-call(bf16[256,256]{1,0:T(8,128)(2,1)} %get-tuple-element.9.pixel, f32[16,256]{1,0:T(8,128)} %get-tuple-element.12.states, f32[256,128]{1,0:T(8,128)} %bitcast.10, bf16[2,256,256]{2,1,0:T(8,128)(2,1)} %w_out.3, f32[1,256]{1,0:T(1,128)} %bitcast.18, ...), custom_call_target="tpu_custom_call" | custom-call | tf_op jit(solution)/shard_map/final_logits/pallas_call | solution.py:353
  (14 shorter events, 0.0 us)
Async XLA Ops:
  0.6 26.9 %copy-start.6 = (s32[16,4]{0,1:T(4,128)S(1)}, s32[16,4]{0,1:T(4,128)}, u32[]{:S(2)}) copy-start(s32[16,4]{0,1:T(4,128)} %param.19) | copy-start | bytes 772
  1.5 5.2 %collective-permute-start.2 = (bf16[128,256]{1,0:T(8,128)(2,1)S(1)}, bf16[128,256]{1,0:T(8,128)(2,1)S(1)}, u32[]{:S(2)}, u32[]{:S(2)}) collective-permute-start(bf16[128,256]{1,0:T(8,128)(2,1)S(1)} %dynamic-slice_bitcast_fusion), channel_id=1, source_target_pairs={{0,1},{1,0},{2,3},{3,2},{4,5},{5,4},{6,7},{7,6},{8,9},{9,8},{10,11... | collective-permute-start | bytes 196616 | tf_op jit(solution)/shard_map/ppermute | solution.py:38
  4.5 9.5 %collective-permute-start = (bf16[2,128,256]{2,1,0:T(8,128)(2,1)}, bf16[2,128,256]{2,1,0:T(8,128)(2,1)S(1)}, u32[]{:S(2)}, u32[]{:S(2)}) collective-permute-start(bf16[2,128,256]{2,1,0:T(8,128)(2,1)} %bitcast.12), channel_id=1, source_target_pairs={{0,2},{1,3},{2,0},{3,1},{4,6},{5,7},{6,4},{7,5},{8,10},{9,11},{10,... | collective-permute-start | bytes 393224 | tf_op jit(solution)/shard_map/ppermute | solution.py:38
  4.5 9.5 %collective-permute-start.1 = (bf16[2,128,256]{2,1,0:T(8,128)(2,1)}, bf16[2,128,256]{2,1,0:T(8,128)(2,1)S(1)}, u32[]{:S(2)}, u32[]{:S(2)}) collective-permute-start(bf16[2,128,256]{2,1,0:T(8,128)(2,1)} %bitcast.13), channel_id=1, source_target_pairs={{2,4},{3,5},{4,2},{5,3},{6,8},{7,9},{8,6},{9,7},{10,12},{11,13},{1... | collective-permute-start | bytes 393224 | tf_op jit(solution)/shard_map/ppermute | solution.py:38
  5.2 8.8 %collective-permute-start.4 = (bf16[128,256]{1,0:T(8,128)(2,1)S(1)}, bf16[128,256]{1,0:T(8,128)(2,1)S(1)}, u32[]{:S(2)}, u32[]{:S(2)}) collective-permute-start(bf16[128,256]{1,0:T(8,128)(2,1)S(1)} %dynamic-slice_bitcast_fusion), channel_id=1, source_target_pairs={{2,5},{3,4},{4,3},{5,2},{6,9},{7,8},{8,7},{9,6},{10,13},{11,12},{1... | collective-permute-start | bytes 196616 | tf_op jit(solution)/shard_map/ppermute | solution.py:38
  6.7 7.3 %copy-start.3 = (bf16[128,256]{1,0:T(8,128)(2,1)}, bf16[128,256]{1,0:T(8,128)(2,1)S(1)}, u32[]{:S(2)}) copy-start(bf16[128,256]{1,0:T(8,128)(2,1)S(1)} %collective-permute-done.2.refs_3_) | copy-start | bytes 196612
  6.7 7.2 %collective-permute-start.3 = (bf16[128,256]{1,0:T(8,128)(2,1)S(1)}, bf16[128,256]{1,0:T(8,128)(2,1)S(1)}, u32[]{:S(2)}, u32[]{:S(2)}) collective-permute-start(bf16[128,256]{1,0:T(8,128)(2,1)S(1)} %collective-permute-done.2.refs_3_), channel_id=1, source_target_pairs={{0,2},{1,3},{2,0},{3,1},{4,6},{5,7},{6,4},{7,5},{8,10},{9,11},{10,... | collective-permute-start | bytes 196616 | tf_op jit(solution)/shard_map/ppermute | solution.py:38
  10.1 3.9 %collective-permute-start.5 = (f32[8,256]{1,0:T(8,128)}, f32[8,256]{1,0:T(8,128)S(1)}, u32[]{:S(2)}, u32[]{:S(2)}) collective-permute-start(f32[8,256]{1,0:T(8,128)} %refs_7_.1), channel_id=1, source_target_pairs={{0,1},{1,0},{2,3},{3,2},{4,5},{5,4},{6,7},{7,6},{8,9},{9,8},{10,11... | collective-permute-start | bytes 24584 | tf_op jit(solution)/shard_map/ppermute | solution.py:38
  14.0 0.6 %copy-start.7 = (f32[8,256]{1,0:T(8,128)}, f32[8,256]{1,0:T(8,128)S(1)}, u32[]{:S(2)}) copy-start(f32[8,256]{1,0:T(8,128)S(1)} %collective-permute-done.5.refs_8_) | copy-start | bytes 24580
  14.0 0.6 %copy-start.4 = (bf16[128,256]{1,0:T(8,128)(2,1)}, bf16[128,256]{1,0:T(8,128)(2,1)S(1)}, u32[]{:S(2)}) copy-start(bf16[128,256]{1,0:T(8,128)(2,1)S(1)} %collective-permute-done.4.refs_5_) | copy-start | bytes 196612
  14.0 0.6 %copy-start.5 = (bf16[128,256]{1,0:T(8,128)(2,1)}, bf16[128,256]{1,0:T(8,128)(2,1)S(1)}, u32[]{:S(2)}) copy-start(bf16[128,256]{1,0:T(8,128)(2,1)S(1)} %collective-permute-done.3.refs_4_) | copy-start | bytes 196612
  14.0 0.7 %copy-start.1 = (bf16[2,128,256]{2,1,0:T(8,128)(2,1)}, bf16[2,128,256]{2,1,0:T(8,128)(2,1)S(1)}, u32[]{:S(2)}) copy-start(bf16[2,128,256]{2,1,0:T(8,128)(2,1)S(1)} %collective-permute-done.refs_1_) | copy-start | bytes 393220
  14.0 0.7 %copy-start.2 = (bf16[2,128,256]{2,1,0:T(8,128)(2,1)}, bf16[2,128,256]{2,1,0:T(8,128)(2,1)S(1)}, u32[]{:S(2)}) copy-start(bf16[2,128,256]{2,1,0:T(8,128)(2,1)S(1)} %collective-permute-done.1.refs_2_) | copy-start | bytes 393220
  21.3 14.8 %all-to-all-start = ((f32[32,8,128]{2,1,0:T(8,128)}), f32[32,8,128]{2,1,0:T(8,128)S(1)}, u32[]{:S(2)}, u32[]{:S(2)}) async-start(f32[32,8,128]{2,1,0:T(8,128)} %broadcast_in_dim.4), calls=%async_computation | async-start | bytes 262144 | tf_op jit(solution)/shard_map/all_to_all | solution.py:262
  36.1 0.7 %copy-start = (f32[32,8,128]{2,1,0:T(8,128)}, f32[32,8,128]{2,1,0:T(8,128)S(1)}, u32[]{:S(2)}) copy-start(f32[32,8,128]{2,1,0:T(8,128)S(1)} %all-to-all-done) | copy-start | bytes 393220

commit v2 on v1

v2 whole, which is shorter than its diff:
```python
import functools

import jax
import jax.numpy as jnp
from jax import lax
from jax.experimental import pallas as pl
from jax.experimental.pallas import tpu as pltpu
from jax.sharding import PartitionSpec as P

HEADS = 8
LAYERS = 2
LANES = 128
SLOTS = 8
PIECES = 3
AXES = ("span", "qry")
F32 = jnp.float32
BF16 = jnp.bfloat16


def iota(dims, dim):
    return lax.broadcasted_iota(jnp.int32, dims, dim)


def swap_partner(index, count, parity):
    other = index ^ 1 if parity == 0 else ((index + 1) ^ 1) - 1
    return other if 0 <= other < count else None


def swap(value, counts, parities):
    pairs = []
    for first in range(counts[0]):
        for second in range(counts[1]):
            ends = [
                index if parity is None else swap_partner(index, count, parity)
                for index, count, parity in zip((first, second), counts, parities)
            ]
            if None not in ends:
                pairs.append((first * counts[1] + second, ends[0] * counts[1] + ends[1]))
    return lax.ppermute(value, AXES, pairs)


def partials(qproj, keys, values, listed, x_cells, slots, out_ref):
    voxels, channels = keys.shape
    blocks = voxels // x_cells
    rows = blocks * HEADS
    head_dim = channels // HEADS
    chosen = jnp.dot(listed, qproj, preferred_element_type=F32)
    own_head = iota((rows, channels), 1) // head_dim == iota((rows, channels), 0) % HEADS
    chosen = jnp.where(own_head, chosen, 0.0).astype(BF16)
    scores = lax.dot_general(chosen, keys, (((1,), (1,)), ((), ())), preferred_element_type=F32)
    allowed = iota((rows, voxels), 1) // x_cells == iota((rows, voxels), 0) // HEADS
    top = jnp.max(jnp.where(allowed, scores, -jnp.inf), axis=1, keepdims=True)
    prob = jnp.where(allowed, jnp.exp(scores - top), 0.0)
    total = jnp.sum(prob, axis=1, keepdims=True)
    weighted = jnp.dot(prob.astype(BF16), values, preferred_element_type=F32)
    weighted = jnp.where(own_head, weighted / total, 0.0)
    rest = top + jnp.log(total)
    lane = iota((rows, LANES), 1)
    head = iota((rows, LANES), 0) % HEADS
    levels = jnp.zeros((rows, LANES), F32)
    for piece in range(PIECES):
        part = rest.astype(BF16).astype(F32)
        rest = rest - part
        levels = jnp.where(lane == head + piece * HEADS, part, levels)
    wide = channels // LANES
    for block in range(blocks):
        span = slice(block * HEADS, (block + 1) * HEADS)
        summed = jnp.sum(weighted[span], axis=0, keepdims=True)
        for part in range(wide):
            row = block * wide + part
            slots[row : row + 1, :] = summed[:, part * LANES : (part + 1) * LANES]
        row = blocks * wide + block
        slots[row : row + 1, :] = jnp.sum(levels[span], axis=0, keepdims=True)
    out_ref[...] = jnp.broadcast_to(slots[...].astype(BF16)[None], out_ref.shape)


def merged(gathered, pick, spread, channels, query_count):
    wide = channels // LANES
    listed = pick.shape[0] // (wide + 1)
    places = listed // query_count
    picked = jnp.dot(pick, gathered, preferred_element_type=F32)
    levels = jnp.dot(picked[wide * listed :].astype(BF16), spread, preferred_element_type=F32)
    sums = jnp.concatenate(
        [picked[part * listed : (part + 1) * listed] for part in range(wide)], axis=1
    )

    def place(value, index):
        return value[index * query_count : (index + 1) * query_count]

    top = functools.reduce(jnp.maximum, [place(levels, index) for index in range(places)])
    weights = [jnp.exp(place(levels, index) - top) for index in range(places)]
    total = sum(weights)
    attn = sum(weight * place(sums, index) for index, weight in enumerate(weights)) / total
    return attn.astype(BF16)


def project(state, w_query, head_dim):
    return (
        jnp.dot(state.astype(BF16), w_query, preferred_element_type=F32) * head_dim ** (-0.5)
    ).astype(BF16)


def early_kernel(
    x_cells,
    own_hbm,
    taps_hbm,
    w_query_hbm,
    w_key_hbm,
    w_value_hbm,
    w_out_hbm,
    mask_weight_hbm,
    mask_rows,
    mask_column,
    taps,
    w_query,
    w_key,
    w_value,
    w_out,
    mask_weight,
    sums,
    listed,
    pick,
    spread,
    own,
    arrived,
):
    per_plane = taps.shape[0] // 3
    middle, low, high = (pl.ds(index * per_plane, per_plane) for index in (1, 0, 2))
    moves = [(own_hbm, own)]
    moves += [(taps_hbm.at[part], taps.at[part]) for part in (middle, low, high)]
    moves += [
        (w_query_hbm, w_query),
        (w_key_hbm, w_key),
        (w_value_hbm, w_value),
        (w_out_hbm, w_out),
        (mask_weight_hbm, mask_weight),
    ]
    copies = [
        pltpu.make_async_copy(source, target, arrived.at[index])
        for index, (source, target) in enumerate(moves)
    ]
    for copy in copies:
        copy.start()
    row_cells, _, channels = own.shape
    blocks = row_cells
    wide = channels // LANES
    query_count = mask_rows.shape[1]
    base = (lax.axis_index("span") * lax.axis_size("qry") + lax.axis_index("qry")) * blocks
    block_of_row = base + iota(listed.shape, 0) // HEADS
    hit = mask_rows[0:1, :] == block_of_row
    for place in range(1, mask_rows.shape[0]):
        hit = hit | (mask_rows[place : place + 1, :] == block_of_row)
    listed[...] = hit.astype(F32).astype(BF16)
    wanted = mask_column[...]
    many = wanted.shape[0]
    first_slot = wanted // blocks * SLOTS
    local_block = wanted % blocks
    slot = iota((many, pick.shape[1]), 1)
    for part in range(wide):
        target = first_slot + local_block * wide + part
        pick[part * many : (part + 1) * many, :] = (slot == target).astype(F32).astype(BF16)
    target = first_slot + blocks * wide + local_block
    pick[wide * many :, :] = (slot == target).astype(F32).astype(BF16)
    lane = iota(spread.shape, 0)
    head = iota(spread.shape, 1) // (channels // HEADS)
    spread[...] = ((lane % HEADS == head) & (lane < PIECES * HEADS)).astype(F32).astype(BF16)
    copies[0].wait()
    copies[1].wait()
    for x_off in range(3):
        total = None
        for row_off in range(3):
            rows = []
            for row in range(row_cells):
                source = row + row_off - 1
                if 0 <= source < row_cells:
                    rows.append(own[source])
                else:
                    rows.append(jnp.zeros(own.shape[1:], BF16))
            slab = jnp.concatenate(rows, axis=0)
            product = jnp.dot(
                slab, taps[per_plane + 3 * row_off + x_off], preferred_element_type=F32
            )
            total = product if total is None else total + product
        sums[x_off] = total
    for copy in copies[2:]:
        copy.wait()


def conv_kernel(sides, *refs):
    (plane_even, plane_odd, *rest) = refs
    halos = rest[: 3 * sides]
    (taps, sums_in, queries, peers, w_query, w_key, w_value, listed) = rest[
        3 * sides : 3 * sides + 8
    ]
    (pixel, states, parts, cells, slots) = rest[3 * sides + 8 :]
    row_cells, x_cells, channels = plane_even.shape
    row_id = lax.axis_index("qry")
    odd = lax.axis_index("span") % 2
    even_plane = 2 - 2 * odd
    odd_plane = 2 * odd
    blank = jnp.zeros((x_cells, channels), BF16)
    for depth_off in range(3):
        cells[depth_off, 0] = blank
        cells[depth_off, row_cells + 1] = blank
    for row in range(row_cells):
        cells[1, row + 1] = blank
        cells[even_plane, row + 1] = plane_even[row]
        cells[odd_plane, row + 1] = plane_odd[row]
    low = row_id % 2 == 0
    for parity in range(sides):
        at_end = low if parity == 0 else jnp.logical_not(low)
        row = jnp.where(at_end, row_cells + 1, 0)
        cells[1, row] = halos[3 * parity][...]
        cells[even_plane, row] = halos[3 * parity + 1][...]
        cells[odd_plane, row] = halos[3 * parity + 2][...]
    voxels = row_cells * x_cells
    sums = [sums_in[x_off] for x_off in range(3)]
    for depth_off in (0, 2, 1):
        for row_off in (0, 2) if depth_off == 1 else range(3):
            slab = cells[depth_off, row_off : row_off + row_cells].reshape(voxels, channels)
            for x_off in range(3):
                sums[x_off] = sums[x_off] + jnp.dot(
                    slab, taps[9 * depth_off + 3 * row_off + x_off], preferred_element_type=F32
                )
    x_id = iota((voxels, channels), 0) % x_cells
    conv = (
        sums[1]
        + jnp.where(x_id == 0, 0.0, pltpu.roll(sums[0], 1, 0))
        + jnp.where(x_id == x_cells - 1, 0.0, pltpu.roll(sums[2], voxels - 1, 0))
    )
    flat = jnp.maximum(conv, 0.0).astype(BF16)
    pixel[...] = flat
    here = queries.shape[0]
    if peers.shape[0] == states.shape[0]:
        states[...] = peers[...]
    else:
        states[pl.ds(pl.multiple_of(row_id * here, here), here), :] = queries[...]
        states[pl.ds(pl.multiple_of((1 - row_id) * here, here), here), :] = peers[...]
    qproj = project(states[...], w_query[0], channels // HEADS)
    keys = jnp.dot(flat, w_key[0], preferred_element_type=F32).astype(BF16)
    values = jnp.dot(flat, w_value[0], preferred_element_type=F32).astype(BF16)
    slots[...] = jnp.zeros(slots.shape, F32)
    partials(qproj, keys, values, listed[...], x_cells, slots, parts)


def layer_kernel(
    layer,
    x_cells,
    pixel,
    states,
    gathered,
    w_out,
    w_query,
    w_key,
    w_value,
    listed,
    pick,
    spread,
    new_states,
    parts,
    slots,
):
    channels = pixel.shape[1]
    flat = pixel[...]
    keys = jnp.dot(flat, w_key[layer], preferred_element_type=F32).astype(BF16)
    values = jnp.dot(flat, w_value[layer], preferred_element_type=F32).astype(BF16)
    attn = merged(gathered[...], pick[...], spread[...], channels, states.shape[0])
    state = states[...] + jnp.dot(attn, w_out[layer - 1], preferred_element_type=F32)
    new_states[...] = state
    qproj = project(state, w_query[layer], channels // HEADS)
    slots[...] = jnp.zeros(slots.shape, F32)
    partials(qproj, keys, values, listed[...], x_cells, slots, parts)


def final_kernel(
    x_cells,
    pixel,
    states,
    gathered,
    w_out,
    norm_gain,
    mask_weight,
    pick,
    spread,
    embed,
    logits,
    all_rows,
):
    voxels, channels = pixel.shape
    attn = merged(gathered[...], pick[...], spread[...], channels, states.shape[0])
    state = states[...] + jnp.dot(attn, w_out[LAYERS - 1], preferred_element_type=F32)
    mean = jnp.mean(state, axis=-1, keepdims=True)
    centered = state - mean
    var = jnp.mean(centered * centered, axis=-1, keepdims=True)
    query_embed = centered * lax.rsqrt(var + 1e-05) * norm_gain[...]
    all_rows[...] = query_embed
    here = embed.shape[0]
    embed[...] = all_rows[pl.ds(pl.multiple_of(lax.axis_index("qry") * here, here), here), :]
    mask_embed = jnp.dot(
        query_embed.astype(BF16), mask_weight[...], preferred_element_type=F32
    ).astype(BF16)
    scores = lax.dot_general(
        mask_embed, pixel[...], (((1,), (1,)), ((), ())), preferred_element_type=F32
    ) * channels ** (-0.5)
    for block in range(voxels // x_cells):
        logits[:, block, :] = scores[:, block * x_cells : (block + 1) * x_cells].astype(BF16)


def shape(dims, dtype):
    return jax.ShapeDtypeStruct(dims, dtype)


VMEM = pl.BlockSpec(memory_space=pltpu.VMEM)
HBM = pl.BlockSpec(memory_space=pltpu.HBM)


def grant(mebibytes):
    return pltpu.CompilerParams(vmem_limit_bytes=mebibytes << 20)


def kernel(body, outs, ins, scratch, room, name):
    return pl.pallas_call(
        body,
        out_shape=outs,
        in_specs=ins,
        out_specs=[VMEM] * len(outs),
        scratch_shapes=scratch,
        compiler_params=grant(room),
        name=name,
    )


def exchange(parts):
    gathered = lax.all_to_all(parts, AXES, split_axis=0, concat_axis=0, tiled=True)
    return gathered.reshape(-1, LANES)


def local(
    counts,
    features,
    conv_weight,
    queries,
    w_query,
    w_key,
    w_value,
    w_out,
    norm_gain,
    mask_weight,
    mask_blocks,
):
    depth_cells, row_cells, x_cells, channels = features.shape
    assert depth_cells == 1
    devices = counts[0] * counts[1]
    query_count, places = mask_blocks.shape
    voxels = row_cells * x_cells
    wide = channels // LANES
    assert row_cells * (wide + 1) <= SLOTS
    rows = row_cells * HEADS
    listed_count = query_count * places
    own = features[0]
    plane_odd = swap(own, counts, (1, None))
    plane_even = swap(own, counts, (0, None))
    row_low = lax.axis_index("qry") % 2 == 0
    halos = []
    parities = (0,) if counts[1] == 2 else (0, 1)
    for parity in parities:
        at_end = row_low if parity == 0 else jnp.logical_not(row_low)
        edge = lax.dynamic_index_in_dim(
            own, jnp.where(at_end, row_cells - 1, 0), axis=0, keepdims=False
        )
        for depth_parity in (None, 0, 1):
            halos.append(swap(edge, counts, (depth_parity, parity)))
    if counts[1] == 2:
        peers = swap(queries, counts, (None, 0))
    else:
        peers = lax.all_gather(queries, "qry", axis=0, tiled=True)
    mask_rows = mask_blocks.T
    mask_column = mask_rows.reshape(listed_count, 1)
    constant = [own, conv_weight, w_query, w_key, w_value, w_out, mask_weight]
    constant = [pltpu.with_memory_space_constraint(value, pltpu.HBM) for value in constant]
    (taps, w_query, w_key, w_value, w_out, mask_weight, sums, listed, pick, spread) = kernel(
        functools.partial(early_kernel, x_cells),
        [shape(value.shape, value.dtype) for value in constant[1:]]
        + [
            shape((3, voxels, channels), F32),
            shape((rows, query_count), BF16),
            shape(((wide + 1) * listed_count, devices * SLOTS), BF16),
            shape((LANES, channels), BF16),
        ],
        [HBM] * len(constant) + [VMEM] * 2,
        [pltpu.VMEM(own.shape, BF16), pltpu.SemaphoreType.DMA((9,))],
        24,
        "early",
    )(*constant, mask_rows, mask_column)
    parts_shape = shape((devices, SLOTS, LANES), BF16)
    slots = pltpu.VMEM((SLOTS, LANES), F32)
    states_shape = shape((query_count, channels), F32)
    pixel, states, parts = kernel(
        functools.partial(conv_kernel, len(parities)),
        [shape((voxels, channels), BF16), states_shape, parts_shape],
        [VMEM] * (10 + len(halos)),
        [pltpu.VMEM((3, row_cells + 2, x_cells, channels), BF16), slots],
        12,
        "conv_partials",
    )(
        plane_even,
        plane_odd,
        *halos,
        taps,
        sums,
        queries,
        peers,
        w_query,
        w_key,
        w_value,
        listed,
    )
    for layer in range(1, LAYERS):
        states, parts = kernel(
            functools.partial(layer_kernel, layer, x_cells),
            [states_shape, parts_shape],
            [VMEM] * 10,
            [slots],
            16,
            "layer_partials",
        )(
            pixel,
            states,
            exchange(parts),
            w_out,
            w_query,
            w_key,
            w_value,
            listed,
            pick,
            spread,
        )
    embed, logits = kernel(
        functools.partial(final_kernel, x_cells),
        [shape(queries.shape, F32), shape((query_count, row_cells, x_cells), BF16)],
        [VMEM] * 8,
        [pltpu.VMEM((query_count, channels), F32)],
        16,
        "final_logits",
    )(
        pixel,
        states,
        exchange(parts),
        w_out,
        norm_gain.reshape(1, channels),
        mask_weight,
        pick,
        spread,
    )
    return embed, logits.reshape(query_count, depth_cells, row_cells, x_cells)


def solution(mesh):
    counts = (mesh.shape["span"], mesh.shape["qry"])
    return jax.shard_map(
        functools.partial(local, counts),
        mesh=mesh,
        in_specs=(
            P("span", "qry", None, None),
            P(),
            P("qry", None),
            P(),
            P(),
            P(),
            P(),
            P(),
            P(),
            P(),
        ),
        out_specs=(P("qry", None), P(None, "span", "qry", None)),
        check_vma=False,
    )
```

time: 54.9 us -> 43.4 us (0.79)
  blocking collectives: 11 us -> 21.5 us
  waiting for transfers between devices: 10.6 us -> 0.13 us
  Pallas kernels: 11.2 us -> 6.72 us
  starting transfers between devices: 15.9 us -> 11.8 us
  local copies, waits for them, and re-layouts: 4.93 us -> 2.29 us
    all_to_all x1 -> x2, blocking collectives: 11 us -> 21.5 us  [exchange(): lax.all_to_all(parts, AXES, split_axis=0, concat_axis=0, tiled=True)]
    all_to_all x1 -> x0, waiting for transfers between devices: 7.88 us -> none  [exchange(): lax.all_to_all(copies, axes, split_axis=0, concat_axis=0, tiled=True)]
    all_to_all x1 -> x0, starting transfers between devices: 6.24 us -> none  [exchange(): lax.all_to_all(copies, axes, split_axis=0, concat_axis=0, tiled=True)]
    pallas_call x3 -> x4, Pallas kernels: 11.2 us -> 6.72 us  [the longest x1 2.44 us: local(): kernel(functools.partial(early_kernel, x_cells), [shape(value.shape, valu...]
    ppermute x6, waiting for transfers between devices: 2.75 us -> 0.13 us  [swap(): return lax.ppermute(value, AXES, pairs)]
    ppermute x6, starting transfers between devices: 9.7 us -> 11.8 us  [swap(): return lax.ppermute(value, AXES, pairs)]
    broadcast_in_dim x2 -> x0, local copies, waits for them, and re-layouts: 2.05 us -> none  [exchange(): copies = jnp.broadcast_to(parts[None], (devices, *parts.shape))]
    unnamed x16 -> x6, local copies, waits for them, and re-layouts: 1.33 us -> 0.69 us
  transfers between devices with their start and end apart: 7 -> 6, of which waited for: 3 -> 1; matrix products, arithmetic and copies ran while one was open for 1% -> 4% of each run, Pallas kernels for 0% -> 6%
where the time goes in v2:
time: 43.4 us; the launch traced here: 43.1 us
  blocking collectives  21.5 us (50%)
  starting transfers between devices  11.8 us (27%)
  Pallas kernels  6.72 us (15%)
  local copies, waits for them, and re-layouts  2.29 us (5%)
  between operations  0.72 us (2%)
    all_to_all x2, blocking collectives, exchange(): lax.all_to_all(parts, AXES, split_axis=0, concat_axis=0, tiled=True)  21.5 us
    ppermute x6, starting transfers between devices, swap(): return lax.ppermute(value, AXES, pairs)  11.8 us
    pallas_call x1, Pallas kernels, local(): kernel(functools.partial(early_kernel, x_cells), [shape(value.shape, valu...  2.44 us
    pallas_call x1, Pallas kernels, local(): kernel(functools.partial(conv_kernel, len(parities)), [shape((voxels, cha...  1.71 us
    pallas_call x1, Pallas kernels, local(): kernel(functools.partial(final_kernel, x_cells), [shape(queries.shape, F3...  1.46 us
    pallas_call x1, Pallas kernels, local(): kernel(functools.partial(layer_kernel, layer, x_cells), [states_shape, pa...  1.1 us
  transfers between devices with their start and end apart: 6, of which 1 were waited for; matrix products, arithmetic and copies ran while one was open for 4% of the time, Pallas kernels for 6%

profile of v2, /device:TPU:0, one launch (start us, length us, event | category | flops | bytes accessed | tf_op | source)
XLA Modules:
  0.0 43.1 jit_solution(17020559339771690721)
XLA Ops:
  0.6 0.7 %collective-permute-start.1 = (bf16[2,128,256]{2,1,0:T(8,128)(2,1)}, bf16[2,128,256]{2,1,0:T(8,128)(2,1)S(1)}, u32[]{:S(2)}, u32[]{:S(2)}) collective-permute-start(bf16[2,128,256]{2,1,0:T(8,128)(2,1)} %bitcast.15), channel_id=1, source_target_pairs={{2,4},{3,5},{4,2},{5,3},{6,8},{7,9},{8,6},{9,7},{10,12},{11,13},{1... | collective-permute-start | bytes 393224 | tf_op jit(solution)/shard_map/ppermute | solution.py:39
  1.3 4.4 %collective-permute-start = (bf16[2,128,256]{2,1,0:T(8,128)(2,1)}, bf16[2,128,256]{2,1,0:T(8,128)(2,1)S(1)}, u32[]{:S(2)}, u32[]{:S(2)}) collective-permute-start(bf16[2,128,256]{2,1,0:T(8,128)(2,1)} %bitcast.16), channel_id=1, source_target_pairs={{0,2},{1,3},{2,0},{3,1},{4,6},{5,7},{6,4},{7,5},{8,10},{9,11},{10,... | collective-permute-start | bytes 393224 | tf_op jit(solution)/shard_map/ppermute | solution.py:39
  5.7 1.5 %collective-permute-start.5 = (f32[8,256]{1,0:T(8,128)}, f32[8,256]{1,0:T(8,128)S(1)}, u32[]{:S(2)}, u32[]{:S(2)}) collective-permute-start(f32[8,256]{1,0:T(8,128)} %refs_7_.1), channel_id=1, source_target_pairs={{0,1},{1,0},{2,3},{3,2},{4,5},{5,4},{6,7},{7,6},{8,9},{9,8},{10,11... | collective-permute-start | bytes 24584 | tf_op jit(solution)/shard_map/ppermute | solution.py:39
  7.2 0.8 %dynamic-slice_bitcast_fusion = bf16[128,256]{1,0:T(8,128)(2,1)S(1)} fusion(bf16[1,2,128,256]{3,2,1,0:T(8,128)(2,1)} %param.10, s32[]{:T(128)S(6)} %select_n.14), kind=kLoop, calls=%fused_computation | loop fusion | bytes 131076 | tf_op jit(solution)/shard_map/jit(dynamic_index_in_dim)/squeeze | solution.py:368
  8.1 0.7 %collective-permute-start.4 = (bf16[128,256]{1,0:T(8,128)(2,1)S(1)}, bf16[128,256]{1,0:T(8,128)(2,1)S(1)}, u32[]{:S(2)}, u32[]{:S(2)}) collective-permute-start(bf16[128,256]{1,0:T(8,128)(2,1)S(1)} %dynamic-slice_bitcast_fusion), channel_id=1, source_target_pairs={{2,5},{3,4},{4,3},{5,2},{6,9},{7,8},{8,7},{9,6},{10,13},{11,12},{1... | collective-permute-start | bytes 196616 | tf_op jit(solution)/shard_map/ppermute | solution.py:39
  8.7 4.0 %collective-permute-start.3 = (bf16[128,256]{1,0:T(8,128)(2,1)S(1)}, bf16[128,256]{1,0:T(8,128)(2,1)S(1)}, u32[]{:S(2)}, u32[]{:S(2)}) collective-permute-start(bf16[128,256]{1,0:T(8,128)(2,1)S(1)} %dynamic-slice_bitcast_fusion), channel_id=1, source_target_pairs={{0,3},{1,2},{2,1},{3,0},{4,7},{5,6},{6,5},{7,4},{8,11},{9,10},{10,... | collective-permute-start | bytes 196616 | tf_op jit(solution)/shard_map/ppermute | solution.py:39
  12.8 0.0 collective-permute-done.5.refs_8_
  12.8 0.5 %collective-permute-start.2 = (bf16[128,256]{1,0:T(8,128)(2,1)S(1)}, bf16[128,256]{1,0:T(8,128)(2,1)S(1)}, u32[]{:S(2)}, u32[]{:S(2)}) collective-permute-start(bf16[128,256]{1,0:T(8,128)(2,1)S(1)} %dynamic-slice_bitcast_fusion), channel_id=1, source_target_pairs={{0,1},{1,0},{2,3},{3,2},{4,5},{5,4},{6,7},{7,6},{8,9},{9,8},{10,11... | collective-permute-start | bytes 196616 | tf_op jit(solution)/shard_map/ppermute | solution.py:39
  13.3 0.8 %reshape.26.mask_column = s32[64,1]{1,0:T(8,128)S(1)} reshape(s32[4,16]{1,0:T(4,128)} %bitcast.12) | data formatting | bytes 512 | tf_op jit(solution)/shard_map/reshape | solution.py:378
  14.1 0.0 copy-start.1
  14.1 0.7 %copy-done.1 = s32[16,4]{0,1:T(4,128)S(1)} copy-done((s32[16,4]{0,1:T(4,128)S(1)}, s32[16,4]{0,1:T(4,128)}, u32[]{:S(2)}) %copy-start.1) | copy-done | bytes 280
  14.7 2.4 %early.1 = (bf16[27,256,256]{2,1,0:T(8,128)(2,1)S(1)}, bf16[2,256,256]{2,1,0:T(8,128)(2,1)S(1)}, bf16[2,256,256]{2,1,0:T(8,128)(2,1)S(1)}, bf16[2,256,256]{2,1,0...) custom-call(bf16[2,128,256]{2,1,0:T(8,128)(2,1)} %bitcast.17, ...), custom_call_target="tpu_custom_call" | custom-call | tf_op jit(solution)/shard_map/early/pallas_call | solution.py:381
  17.2 0.0 collective-permute-done.4.refs_4_
  17.2 0.0 collective-permute-done.3.refs_3_
  17.2 0.1 collective-permute-done.2.refs_2_
  17.3 0.0 collective-permute-done.1.refs_1_
  17.3 0.0 collective-permute-done.refs_0_
  17.3 0.0 copy-done
  17.3 0.0 copy-start.2
  17.4 1.7 %conv_partials.1 = (bf16[256,256]{1,0:T(8,128)(2,1)S(1)}, f32[16,256]{1,0:T(8,128)S(1)}, bf16[32,8,128]{2,1,0:T(8,128)(2,1)S(1)}) custom-call(bf16[2,128,256]{2,1,0:T(8,128)(2,1)S(1)} %collective-permute-done.refs_0_, bf16[2,128,256]{2,1,0:T(8,128)(2,1)S(1)} %collective-permute-done.1.refs_1_, bf16[128,256]{1,0:T(8,128)(2,1)S(1)} %collective-permute-done.2.refs_2_, ...), custom_call_target="tpu_custom_call" | custom-call | tf_op jit(solution)/shard_map/conv_partials/pallas_call | solution.py:398
  19.1 12.2 %all_to_all.10 = bf16[32,8,128]{2,1,0:T(8,128)(2,1)S(1)} all-to-all(bf16[32,8,128]{2,1,0:T(8,128)(2,1)S(1)} %get-tuple-element.27), channel_id=1, replica_groups=mesh['span'=16,'qry'=2] {'span','qry'}, dimensions={0} | all-to-all | bytes 131072 | tf_op jit(solution)/shard_map/all_to_all | solution.py:334
  31.2 1.1 %layer_partials.1 = (f32[16,256]{1,0:T(8,128)S(1)}, bf16[32,8,128]{2,1,0:T(8,128)(2,1)S(1)}) custom-call(bf16[256,256]{1,0:T(8,128)(2,1)S(1)} %get-tuple-element.25.pixel, f32[16,256]{1,0:T(8,128)S(1)} %get-tuple-element.26.states, bf16[256,128]{1,0:T(8,128)(2,1)S(1)} %bitcast.11, bf16[2,256,256]{2,1,0:T(8,128)(2,1)S(1)} %get-tuple-element.28.w_out, ...), custom_call_target="tpu_custom_call" | custom-call | tf_op jit(solution)/shard_map/layer_partials/pallas_call | solution.py:419
  32.3 9.3 %all_to_all.11 = bf16[32,8,128]{2,1,0:T(8,128)(2,1)S(1)} all-to-all(bf16[32,8,128]{2,1,0:T(8,128)(2,1)S(1)} %get-tuple-element.32), channel_id=1, replica_groups=mesh['span'=16,'qry'=2] {'span','qry'}, dimensions={0} | all-to-all | bytes 131072 | tf_op jit(solution)/shard_map/all_to_all | solution.py:334
  41.6 1.5 %final_logits.1 = (f32[8,256]{1,0:T(8,128)}, bf16[16,2,128]{2,1,0:T(2,128)(2,1)}) custom-call(bf16[256,256]{1,0:T(8,128)(2,1)S(1)} %get-tuple-element.25.pixel, f32[16,256]{1,0:T(8,128)S(1)} %get-tuple-element.31.states, bf16[256,128]{1,0:T(8,128)(2,1)S(1)} %bitcast.10, bf16[2,256,256]{2,1,0:T(8,128)(2,1)S(1)} %get-tuple-element.28.w_out, ...), custom_call_target="tpu_custom_call" | custom-call | tf_op jit(solution)/shard_map/final_logits/pallas_call | solution.py:438
  (2 shorter events, 0.0 us)
Async XLA Ops:
  0.6 16.7 %copy-start = (f32[8,256]{1,0:T(8,128)S(1)}, f32[8,256]{1,0:T(8,128)}, u32[]{:S(2)}) copy-start(f32[8,256]{1,0:T(8,128)} %refs_7_.1) | copy-start | bytes 24580
  0.6 16.7 %collective-permute-start.1 = (bf16[2,128,256]{2,1,0:T(8,128)(2,1)}, bf16[2,128,256]{2,1,0:T(8,128)(2,1)S(1)}, u32[]{:S(2)}, u32[]{:S(2)}) collective-permute-start(bf16[2,128,256]{2,1,0:T(8,128)(2,1)} %bitcast.15), channel_id=1, source_target_pairs={{2,4},{3,5},{4,2},{5,3},{6,8},{7,9},{8,6},{9,7},{10,12},{11,13},{1... | collective-permute-start | bytes 393224 | tf_op jit(solution)/shard_map/ppermute | solution.py:39
  1.3 16.0 %collective-permute-start = (bf16[2,128,256]{2,1,0:T(8,128)(2,1)}, bf16[2,128,256]{2,1,0:T(8,128)(2,1)S(1)}, u32[]{:S(2)}, u32[]{:S(2)}) collective-permute-start(bf16[2,128,256]{2,1,0:T(8,128)(2,1)} %bitcast.16), channel_id=1, source_target_pairs={{0,2},{1,3},{2,0},{3,1},{4,6},{5,7},{6,4},{7,5},{8,10},{9,11},{10,... | collective-permute-start | bytes 393224 | tf_op jit(solution)/shard_map/ppermute | solution.py:39
  5.7 7.1 %collective-permute-start.5 = (f32[8,256]{1,0:T(8,128)}, f32[8,256]{1,0:T(8,128)S(1)}, u32[]{:S(2)}, u32[]{:S(2)}) collective-permute-start(f32[8,256]{1,0:T(8,128)} %refs_7_.1), channel_id=1, source_target_pairs={{0,1},{1,0},{2,3},{3,2},{4,5},{5,4},{6,7},{7,6},{8,9},{9,8},{10,11... | collective-permute-start | bytes 24584 | tf_op jit(solution)/shard_map/ppermute | solution.py:39
  8.1 9.1 %collective-permute-start.4 = (bf16[128,256]{1,0:T(8,128)(2,1)S(1)}, bf16[128,256]{1,0:T(8,128)(2,1)S(1)}, u32[]{:S(2)}, u32[]{:S(2)}) collective-permute-start(bf16[128,256]{1,0:T(8,128)(2,1)S(1)} %dynamic-slice_bitcast_fusion), channel_id=1, source_target_pairs={{2,5},{3,4},{4,3},{5,2},{6,9},{7,8},{8,7},{9,6},{10,13},{11,12},{1... | collective-permute-start | bytes 196616 | tf_op jit(solution)/shard_map/ppermute | solution.py:39
  8.7 8.5 %collective-permute-start.3 = (bf16[128,256]{1,0:T(8,128)(2,1)S(1)}, bf16[128,256]{1,0:T(8,128)(2,1)S(1)}, u32[]{:S(2)}, u32[]{:S(2)}) collective-permute-start(bf16[128,256]{1,0:T(8,128)(2,1)S(1)} %dynamic-slice_bitcast_fusion), channel_id=1, source_target_pairs={{0,3},{1,2},{2,1},{3,0},{4,7},{5,6},{6,5},{7,4},{8,11},{9,10},{10,... | collective-permute-start | bytes 196616 | tf_op jit(solution)/shard_map/ppermute | solution.py:39
  12.8 4.6 %collective-permute-start.2 = (bf16[128,256]{1,0:T(8,128)(2,1)S(1)}, bf16[128,256]{1,0:T(8,128)(2,1)S(1)}, u32[]{:S(2)}, u32[]{:S(2)}) collective-permute-start(bf16[128,256]{1,0:T(8,128)(2,1)S(1)} %dynamic-slice_bitcast_fusion), channel_id=1, source_target_pairs={{0,1},{1,0},{2,3},{3,2},{4,5},{5,4},{6,7},{7,6},{8,9},{9,8},{10,11... | collective-permute-start | bytes 196616 | tf_op jit(solution)/shard_map/ppermute | solution.py:39
  14.1 0.7 %copy-start.1 = (s32[16,4]{0,1:T(4,128)S(1)}, s32[16,4]{0,1:T(4,128)}, u32[]{:S(2)}) copy-start(s32[16,4]{0,1:T(4,128)} %param.19) | copy-start | bytes 772
  17.3 24.3 %copy-start.2 = (f32[256]{0:T(256)S(1)}, f32[256]{0:T(256)}, u32[]{:S(2)}) copy-start(f32[256]{0:T(256)} %param.17) | copy-start | bytes 3076
